TPU v7x, 128 devices: a whole 4x4x4 slice. The times are simulated.
128 devices in a mesh: ctx: 32 (over z, x, core), tp: 4 (over y).
Axes of the slice: x: 4, y: 4, z: 4, core: 2. Of those that a mesh axis runs over, the one named last changes fastest.
Arguments:
- tokens: bfloat16 [4096, 4096], P('ctx', 'tp'), may hold values from -6 to 6
- in_weight: bfloat16 [4096, 3, 4096], P('ctx', None, 'tp'), may hold values from -0.09375 to 0.09375
- conv_taps: float32 [3, 3, 4096], P(None, None, 'tp'), may hold values from -2.5 to 2.5
- decay_rate: float32 [16, 4096], P(None, 'tp'), may hold values from 0 to 0.034, as said below
- residue: float32 [16, 4096], P(None, 'tp'), may hold values from -1 to 1
- skip: float32 [4096], P('tp'), may hold values from -1 to 1
Outputs:
- mixed: bfloat16 [4096, 4096], P('ctx', 'tp')
Inputs may be any that keep to these rules, and one draw needn't show every extreme that they name: `decay_rate`: positive decay rates of the poles.
All inputs are finite; a program needn't handle non-finite values.
Results may differ from a plain program's by a relative error of at most 0.0063.
Values may be sent and summed in bfloat16 or wider, within the bound.
A program may use at most 128 MiB of HBM per device.

v0:
```python
import math
import jax
import jax.numpy as jnp
from jax import lax
from jax.sharding import PartitionSpec as P


def passed_along(array, axis, by):
    peers = lax.axis_size(axis)
    pairs = [(i, i + by) for i in range(peers) if 0 <= i + by < peers]
    return lax.ppermute(array, axis, pairs)


def entering(array, axis, combine, identity):
    peers, here = (lax.axis_size(axis), lax.axis_index(axis))
    everything = jax.tree.map(lambda part: lax.all_gather(part, axis), array)
    start = jax.tree.map(
        lambda part, zero: jnp.broadcast_to(jnp.asarray(zero, part.dtype), part.shape),
        array,
        identity,
    )

    def turn(k, before):
        reached = k < here
        new = combine(before, jax.tree.map(lambda part: part[k], everything))
        return jax.tree.map(lambda a, b: jnp.where(reached, a, b), new, before)

    return lax.fori_loop(0, peers, turn, start)


def link(earlier, later):
    return (earlier[0] * later[0], later[0] * earlier[1] + later[1])


def per_device(tokens, in_weight, conv_taps, decay_rate, residue, skip):
    rows = tokens.shape[0]
    chans = in_weight.shape[2]
    whole = lax.all_gather(tokens, "tp", axis=1, tiled=True)
    piece = lax.all_gather(in_weight, "ctx", axis=0, tiled=True)
    sums = tuple(
        (jnp.dot(whole, piece[:, g, :], preferred_element_type=jnp.float32) for g in range(3))
    )
    projected = jnp.stack([total.astype(jnp.bfloat16) for total in sums], axis=0)
    edge_out = passed_along(projected[:, rows - 2 :, :], "ctx", 1)
    extended = jnp.concatenate([edge_out, projected], axis=1)
    values = lax.optimization_barrier(extended).astype(jnp.float32)
    filtered = (
        conv_taps[0][:, None, :] * values[:, 2:, :]
        + conv_taps[1][:, None, :] * values[:, 1:-1, :]
        + conv_taps[2][:, None, :] * values[:, :-2, :]
    )
    query = filtered[0]
    gated = filtered[1] * filtered[2]
    span = math.gcd(rows, 32)
    blocks = rows // span
    offsets = jnp.arange(span, dtype=jnp.float32)
    powers = jnp.exp(-decay_rate[None] * offsets[:, None, None])
    response = jnp.sum(residue[None] * powers, axis=1)
    lags = jnp.arange(span)[:, None] - jnp.arange(span)[None, :]
    toeplitz = jnp.where((lags >= 0)[:, :, None], response[jnp.clip(lags, 0, span - 1)], 0.0)
    blocked = gated.reshape(blocks, span, chans)
    inside = jnp.einsum("tsc,bsc->btc", toeplitz, blocked, precision=lax.Precision.HIGHEST)
    tails = jnp.exp(-decay_rate[None] * (span - 1.0 - offsets)[:, None, None])
    ends = jnp.einsum("spc,bsc->bpc", tails, blocked, precision=lax.Precision.HIGHEST)
    block_decay = jnp.broadcast_to(jnp.exp(-decay_rate * span)[None], ends.shape)
    after = lax.associative_scan(link, (block_decay, ends), axis=0)[1]
    final = after[blocks - 1]
    starts = jnp.concatenate([jnp.zeros_like(after[:1]), after[: blocks - 1]], axis=0)
    segment = jnp.exp(-decay_rate * rows)
    carried = entering(
        (segment, final), "ctx", link, (jnp.ones_like(final), jnp.zeros_like(final))
    )[1]
    block_starts = (span * jnp.arange(blocks, dtype=jnp.float32))[:, None, None]
    begin = starts + jnp.exp(-decay_rate[None] * block_starts) * carried[None]
    leading = residue[None] * jnp.exp(-decay_rate[None] * (offsets + 1.0)[:, None, None])
    convolved = inside + jnp.einsum("tpc,bpc->btc", leading, begin, precision=lax.Precision.HIGHEST)
    convolved = convolved.reshape(rows, chans)
    return (query * (convolved + skip[None, :] * gated)).astype(jnp.bfloat16)


def solution(mesh):
    placed = (
        P("ctx", "tp"),
        P("ctx", None, "tp"),
        P(None, None, "tp"),
        P(None, "tp"),
        P(None, "tp"),
        P("tp"),
    )
    return jax.shard_map(
        per_device, mesh=mesh, in_specs=placed, out_specs=P("ctx", "tp"), check_vma=False
    )
```

profile of v0, /device:TPU:32, one launch (start us, length us, event | category | flops | bytes accessed | tf_op | source)
XLA Modules:
  0.0 293.2 jit_solution(15202066247814389937)
XLA Ops:
  6.5 0.7 all-gather.6.cloned.1.call-update
  7.3 0.7 all-gather.8.cloned.1.call-update
  8.1 1.5 multiply_exponential_fusion
  9.6 0.8 slice_bitcast_fusion.21
  10.4 24.7 %all-gather.6.cloned.1.call-done = bf16[128,4096]{1,0:T(8,128)(2,1)} async-done(((bf16[128,1024]{1,0:T(8,128)(2,1)}), bf16[128,4096]{1,0:T(8,128)(2,1)}) %all-gather.6.cloned.1.call-update) | async-done | bytes 1048592 | tf_op jit(solution)/shard_map/all_gather | solution.py:38
  35.1 94.1 %all-gather.8.cloned.1.call-done = bf16[4096,3,1024]{2,0,1:T(8,128)(2,1)} async-done(((bf16[128,3,1024]{2,0,1:T(8,128)(2,1)}), bf16[4096,3,1024]{2,0,1:T(8,128)(2,1)}) %all-gather.8.cloned.1.call-update) | async-done | bytes 25165840 | tf_op jit(solution)/shard_map/all_gather | solution.py:39
  129.2 5.0 %fusion.27 = bf16[1,128,1024]{2,1,0:T(8,128)(2,1)S(1)} fusion(bf16[128,4096]{1,0:T(8,128)(2,1)} %all-gather.6.cloned.1.call-done, bf16[4096,3,1024]{2,0,1:T(8,128)(2,1)} %all-gather.8.cloned.1.call-done), kind=kOutput, calls=%fused_computation.36 | convolution fusion | flops 1073872896 | bytes 9699328 | tf_op jit(solution)/shard_map/dot_general | solution.py:41
  134.1 4.6 %fusion.28 = bf16[1,128,1024]{2,1,0:T(8,128)(2,1)S(1)} fusion(bf16[128,4096]{1,0:T(8,128)(2,1)S(1)} %copy-done.15, bf16[4096,3,1024]{2,0,1:T(8,128)(2,1)} %all-gather.8.cloned.1.call-done), kind=kOutput, calls=%fused_computation.37 | convolution fusion | flops 1073872896 | bytes 9699328 | tf_op jit(solution)/shard_map/dot_general | solution.py:41
  138.8 4.7 %fusion.29 = bf16[1,128,1024]{2,1,0:T(8,128)(2,1)S(1)} fusion(bf16[128,4096]{1,0:T(8,128)(2,1)S(1)} %copy-done.15, bf16[4096,3,1024]{2,0,1:T(8,128)(2,1)} %all-gather.8.cloned.1.call-done), kind=kOutput, calls=%fused_computation.38 | convolution fusion | flops 1073872896 | bytes 9699328 | tf_op jit(solution)/shard_map/dot_general | solution.py:41
  143.5 2.4 collective-permute-start
  145.9 0.2 copy.62
  146.1 4.6 %collective-permute-done = bf16[3,2,1024]{2,1,0:T(2,128)(2,1)S(1)} collective-permute-done((bf16[3,2,1024]{2,1,0:T(2,128)(2,1)S(1)}, bf16[3,2,1024]{2,1,0:T(2,128)(2,1)S(1)}, u32[]{:S(2)}, u32[]{:S(2)}) %collective-permute-start) | collective-permute-done | bytes 12320 | tf_op jit(solution)/shard_map/ppermute | solution.py:11
  150.7 0.2 maximum_maximum_fusion
  150.9 0.2 convert_element_type.18
  151.1 0.5 fusion.22
  151.6 1.1 copy-done
  152.7 0.8 copy.65
  153.5 14.8 %fusion.10 = f32[1024,4,16]{2,1,0:T(4,128)} fusion(f32[4,32,1024]{1,0,2:T(4,128)S(1)} %copy.65, f32[32]{0:T(128)S(1)} %iota_subtract_fusion, f32[16,1024]{0,1:T(8,128)S(1)} %copy.62), kind=kOutput, calls=%fused_computation.16 | convolution fusion | flops 25690112 | bytes 852096 | tf_op jit(solution)/shard_map/spc,bsc->bpc/dot_general | solution.py:64
  168.4 1.9 copy.67
  170.4 0.6 slice.182
  171.1 1.0 copy.61
  172.2 15.3 %multiply_reduce_fusion = f32[32,1024]{0,1:T(8,128)S(1)} fusion(f32[16,1024]{0,1:T(8,128)S(1)} %copy.62, f32[16,1024]{0,1:T(8,128)} %copy.61), kind=kLoop, calls=%fused_computation.20 | loop fusion | flops 1540096 | bytes 262144 | tf_op jit(solution)/shard_map/reduce_sum | solution.py:58
  187.7 5.4 %gather_fusion = f32[1024,1024]{1,0:T(8,128)} fusion(f32[32,1024]{1,0:T(8,128)S(1)} %copy.63, s32[1024]{0:T(1024)S(1)} %broadcast_clamp_fusion), kind=kCustom, calls=%fused_computation | custom fusion | bytes 8392704 | tf_op jit(solution)/shard_map/gather | solution.py:60
  193.2 14.4 %copy.64 = f32[32,32,1024]{1,0,2:T(8,128)} copy(f32[32,32,1024]{2,1,0:T(8,128)} %bitcast.79) | data formatting | bytes 8388608 | tf_op jit(solution)/shard_map/gather | solution.py:60
  207.7 0.7 slice_add_fusion
  208.4 29.5 %fusion.1 = f32[1024,4,32]{2,1,0:T(4,128)} fusion(f32[4,32,1024]{1,0,2:T(4,128)S(1)} %copy.65, f32[32,32,1024]{1,0,2:T(8,128)} %copy.64, pred[32,32]{1,0:T(8,128)(4,1)S(1)} %subtract_compare_fusion), kind=kOutput, calls=%fused_computation.4 | convolution fusion | flops 51380224 | bytes 5243904 | tf_op jit(solution)/shard_map/tsc,bsc->btc/dot_general | solution.py:62
  238.0 30.1 %while.14 = (s32[]{:T(128)}, f32[16,1024]{1,0:T(8,128)S(1)}, s32[]{:T(128)}, f32[32,16,1024]{2,1,0:T(8,128)}, f32[32,16,1024]{2,1,0:T(8,128)}, /*index=5*/s32[]{:T(128)}, s32[]{:T(128)}) while((s32[]{:T(128)}, f32[16,1024]{1,0:T(8,128)S(1)}, s32[]{:T(128)}, f32[32,16,1024]{2,1,0:T(8,128)}, f32[32,16,1024]{2,1,0:T(8,128)}, ...), condition=%wide.region_2.3_spmd.clone, body=%wide.region_1.2_spmd.clone.sunk | while | flops 65540 | bytes 262253 | solution.py:28
  238.0 1.1 fusion.45
  239.1 0.9 fusion.45
  240.0 0.9 fusion.45
  241.0 0.9 fusion.45
  241.9 0.9 fusion.45
  242.8 0.9 fusion.45
  243.8 0.9 fusion.45
  244.7 0.9 fusion.45
  245.7 0.9 fusion.45
  246.6 0.9 fusion.45
  247.5 0.9 fusion.45
  248.5 0.9 fusion.45
  249.4 0.9 fusion.45
  250.3 0.9 fusion.45
  251.3 0.9 fusion.45
  252.2 0.9 fusion.45
  253.2 0.9 fusion.45
  254.1 0.9 fusion.45
  255.0 0.9 fusion.45
  256.0 0.9 fusion.45
  256.9 0.9 fusion.45
  257.8 0.9 fusion.45
  258.8 0.9 fusion.45
  259.7 0.9 fusion.45
  260.6 0.9 fusion.45
  261.6 0.9 fusion.45
  262.5 0.9 fusion.45
  263.5 0.9 fusion.45
  264.4 0.9 fusion.45
  265.3 0.9 fusion.45
  266.3 0.9 fusion.45
  267.2 0.9 fusion.45
  268.1 1.0 multiply_add_fusion
  269.2 1.7 copy.68
  270.9 12.9 %add_bitcast_fusion = f32[4,32,1024]{1,0,2:T(4,128)} fusion(f32[1024,4,32]{2,1,0:T(4,128)S(1)} %copy-done.2, f32[4,16,1024]{1,0,2:T(4,128)} %copy.68, f32[32]{0:T(128)S(1)} %iota_add_fusion, f32[16,1024]{0,1:T(8,128)S(1)} %copy.62, f32[16,1024]{0,1:T(8,128)S(1)} %copy-done.3), kind=kOutput, calls=%fused_computation.27 | convolution fusion | flops 26345472 | bytes 1441920 | tf_op jit(solution)/shard_map/tpc,bpc->btc/dot_general | solution.py:76
  283.8 2.0 copy.69
  285.8 0.9 fusion.31
  (58 shorter events, 0.8 us)
Async XLA Ops:
  6.5 28.5 %all-gather.6.cloned.1.call-start = ((), (), s32[]{:S(2)}) async-start(), calls=%async_computation | async-start | bytes 1310720 | tf_op jit(solution)/shard_map/all_gather | solution.py:38
  7.3 121.9 %all-gather.8.cloned.1.call-start = ((), (), s32[]{:S(2)}) async-start(), calls=%async_computation.1 | async-start | bytes 25952256 | tf_op jit(solution)/shard_map/all_gather | solution.py:39
  8.0 230.0 %all-gather.12.cloned.1.call-start = ((), (), s32[]{:S(2)}) async-start(), calls=%async_computation.3 | async-start | bytes 2162688 | tf_op jit(solution)/shard_map/all_gather | solution.py:16
  9.5 136.3 %copy-start.11 = (f32[16,1024]{1,0:T(8,128)}, f32[16,1024]{1,0:T(8,128)S(1)}, u32[]{:S(2)}) copy-start(f32[16,1024]{1,0:T(8,128)S(1)} %get-tuple-element.144) | copy-start | bytes 196612
  9.6 228.4 %all-gather.10.cloned.1.call-start = ((), (), s32[]{:S(2)}) async-start(), calls=%async_computation.2 | async-start | bytes 2162688 | tf_op jit(solution)/shard_map/all_gather | solution.py:16
  35.1 99.1 %copy-start.15 = (bf16[128,4096]{1,0:T(8,128)(2,1)S(1)}, bf16[128,4096]{1,0:T(8,128)(2,1)}, u32[]{:S(2)}) copy-start(bf16[128,4096]{1,0:T(8,128)(2,1)} %all-gather.6.cloned.1.call-done) | copy-start | bytes 3145732
  143.5 7.2 %collective-permute-start = (bf16[3,2,1024]{2,1,0:T(2,128)(2,1)S(1)}, bf16[3,2,1024]{2,1,0:T(2,128)(2,1)S(1)}, u32[]{:S(2)}, u32[]{:S(2)}) collective-permute-start(bf16[3,2,1024]{2,1,0:T(2,128)(2,1)S(1)} %pad_maximum_fusion.1), channel_id=1, source_target_pairs={{0,4},{4,8},{8,12},{12,16},{16,20},{20,24},{24,28},{28,32},{32,36}... | collective-permute-start | bytes 36872 | tf_op jit(solution)/shard_map/ppermute | solution.py:11
  151.6 1.1 copy-start
  168.4 1.9 copy-start.6
  168.4 2.7 copy-start.13
  170.3 0.8 copy-start.4
  170.4 0.7 copy-start.7
  170.4 0.8 copy-start.9
  193.1 14.5 %copy-start.5 = (f32[1024,4,16]{0,2,1:T(8,128)S(1)}, f32[1024,4,16]{0,2,1:T(8,128)}, u32[]{:S(2)}) copy-start(f32[1024,4,16]{0,2,1:T(8,128)} %copy-done.4) | copy-start | bytes 786436
  193.1 14.5 %copy-start.8 = (f32[1,16,1024]{2,1,0:T(8,128)S(1)}, f32[1,16,1024]{2,1,0:T(8,128)}, u32[]{:S(2)}) copy-start(f32[1,16,1024]{2,1,0:T(8,128)} %copy-done.7) | copy-start | bytes 196612
  193.1 14.5 %copy-start.10 = (f32[1,16,1024]{2,1,0:T(8,128)S(1)}, f32[1,16,1024]{2,1,0:T(8,128)}, u32[]{:S(2)}) copy-start(f32[1,16,1024]{2,1,0:T(8,128)} %copy-done.9) | copy-start | bytes 196612
  208.4 59.7 %copy-start.12 = (f32[16,1024]{1,0:T(8,128)S(1)}, f32[16,1024]{1,0:T(8,128)}, u32[]{:S(2)}) copy-start(f32[16,1024]{1,0:T(8,128)} %copy-done.11) | copy-start | bytes 196612
  238.0 32.9 %copy-start.2 = (f32[1024,4,32]{2,1,0:T(4,128)S(1)}, f32[1024,4,32]{2,1,0:T(4,128)}, u32[]{:S(2)}) copy-start(f32[1024,4,32]{2,1,0:T(4,128)} %fusion.1) | copy-start | bytes 1572868
  238.0 32.9 %copy-start.3 = (f32[16,1024]{0,1:T(8,128)S(1)}, f32[16,1024]{0,1:T(8,128)}, u32[]{:S(2)}) copy-start(f32[16,1024]{0,1:T(8,128)} %copy.61) | copy-start | bytes 196612
  283.8 2.0 copy-start.1
  283.8 2.0 copy-start.14
Sparse Core Ops, SparseCore 0:
  9.0 25.9 all-gather.5
  37.4 91.7 all-gather.7
  131.4 43.6 all-gather.11
  177.3 43.2 all-gather.9
where the time goes:
time: 295 us; the launch traced here: 293 us
  waiting for transfers between devices  125 us (42%)
  matrix products  71.5 us (24%)
  other arithmetic  49.9 us (17%)
  local copies, waits for them, and re-layouts  30.4 us (10%)
  between operations  13.5 us (5%)
    all_gather x1, waiting for transfers between devices, per_device(): piece = lax.all_gather(in_weight, 'ctx', axis=0, tiled=True)  94.1 us
    dot_general x1, matrix products, per_device(): jnp.einsum('tsc,bsc->btc', toeplitz, blocked, precision=lax.Precision.HIG...  29.5 us
    select_n x32, other arithmetic, turn(): return jax.tree.map(lambda a, b: jnp.where(reached, a, b), new, before)  29.4 us
    all_gather x1, waiting for transfers between devices, per_device(): whole = lax.all_gather(tokens, 'tp', axis=1, tiled=True)  24.7 us
    gather x2, local copies, waits for them, and re-layouts, per_device(): response[jnp.clip(lags, 0, span - 1)]  19.8 us
    reduce_sum x1, other arithmetic, per_device(): response = jnp.sum(residue[None] * powers, axis=1)  15.3 us
    dot_general x1, matrix products, per_device(): jnp.einsum('spc,bsc->bpc', tails, blocked, precision=lax.Precision.HIGHEST)  14.8 us
    dot_general x3, matrix products, per_device(): jnp.dot(whole, piece[:, g, :], preferred_element_type=jnp.float32)  14.3 us
  transfers between devices with their start and end apart: 5, of which 3 were waited for; matrix products, arithmetic and copies ran while one was open for 35% of the time, Pallas kernels for 0%

commit v1 on v0

--- a/solution.py
+++ b/solution.py
@@ -1,8 +1,19 @@
+import functools
 import math
 import jax
 import jax.numpy as jnp
 from jax import lax
 from jax.sharding import PartitionSpec as P
+
+
+def pack_task(target, axis_tag):
+    b_now = jnp.stack([target for _ in range(lax.axis_size(axis_tag))])
+    shaped = lax.all_to_all(b_now, axis_tag, 0, 0)
+    u_next = jnp.concatenate(shaped, 1)
+    return u_next
+
+
+meet_lanes = functools.partial(pack_task, axis_tag="tp")
 
 
 def passed_along(array, axis, by):
@@ -35,7 +46,7 @@
 def per_device(tokens, in_weight, conv_taps, decay_rate, residue, skip):
     rows = tokens.shape[0]
     chans = in_weight.shape[2]
-    whole = lax.all_gather(tokens, "tp", axis=1, tiled=True)
+    whole = meet_lanes(tokens)
     piece = lax.all_gather(in_weight, "ctx", axis=0, tiled=True)
     sums = tuple(
         (jnp.dot(whole, piece[:, g, :], preferred_element_type=jnp.float32) for g in range(3))

time: 295 us -> 269 us (0.912)
  waiting for transfers between devices: 125 us -> 93.6 us
  starting transfers between devices: 2.47 us -> 6.87 us
    all_gather x1 -> x0, waiting for transfers between devices: 24.7 us -> none  [per_device(): whole = lax.all_gather(tokens, 'tp', axis=1, tiled=True)]
    all_gather x1, waiting for transfers between devices: 94.1 us -> 74.1 us  [per_device(): piece = lax.all_gather(in_weight, 'ctx', axis=0, tiled=True)]
    all_to_all x0 -> x1, waiting for transfers between devices: none -> 14.3 us  [pack_task(): shaped = lax.all_to_all(b_now, axis_tag, 0, 0)]
    all_to_all x0 -> x1, starting transfers between devices: none -> 4.46 us  [pack_task(): shaped = lax.all_to_all(b_now, axis_tag, 0, 0)]
  transfers between devices with their start and end apart: 5 -> 5, of which waited for: 3 -> 3; matrix products, arithmetic and copies ran while one was open for 35% -> 39% of each run, Pallas kernels for 0% -> 0%
where the time goes in v1:
time: 269 us; the launch traced here: 267 us
  waiting for transfers between devices  93.6 us (35%)
  matrix products  71.3 us (27%)
  other arithmetic  49.1 us (18%)
  local copies, waits for them, and re-layouts  32 us (12%)
  between operations  13.5 us (5%)
  starting transfers between devices  6.87 us (3%)
    all_gather x1, waiting for transfers between devices, per_device(): piece = lax.all_gather(in_weight, 'ctx', axis=0, tiled=True)  74.1 us
    dot_general x1, matrix products, per_device(): jnp.einsum('tsc,bsc->btc', toeplitz, blocked, precision=lax.Precision.HIG...  29.5 us
    select_n x32, other arithmetic, turn(): return jax.tree.map(lambda a, b: jnp.where(reached, a, b), new, before)  29.4 us
    gather x2, local copies, waits for them, and re-layouts, per_device(): response[jnp.clip(lags, 0, span - 1)]  19.9 us
    reduce_sum x1, other arithmetic, per_device(): response = jnp.sum(residue[None] * powers, axis=1)  15.3 us
    dot_general x1, matrix products, per_device(): jnp.einsum('spc,bsc->bpc', tails, blocked, precision=lax.Precision.HIGHEST)  14.8 us
    all_to_all x1, waiting for transfers between devices, pack_task(): shaped = lax.all_to_all(b_now, axis_tag, 0, 0)  14.3 us
    dot_general x3, matrix products, per_device(): jnp.dot(whole, piece[:, g, :], preferred_element_type=jnp.float32)  14 us
  transfers between devices with their start and end apart: 5, of which 3 were waited for; matrix products, arithmetic and copies ran while one was open for 39% of the time, Pallas kernels for 0%

profile of v1, /device:TPU:32, one launch (start us, length us, event | category | flops | bytes accessed | tf_op | source)
XLA Modules:
  0.0 267.0 jit_solution(7396639220630744042)
XLA Ops:
  6.5 0.7 all-gather.5.cloned.1.call-update
  7.3 1.1 copy.64
  8.4 1.1 stack.19
  9.6 4.5 %all-to-all-start = ((bf16[4,128,1024]{1,2,0:T(8,128)(2,1)}), bf16[4,128,1024]{1,2,0:T(8,128)(2,1)S(1)}, u32[]{:S(2)}, u32[]{:S(2)}) async-start(bf16[4,128,1024]{1,2,0:T(8,128)(2,1)} %stack.19), calls=%async_computation | async-start | bytes 2097152 | tf_op jit(solution)/shard_map/all_to_all | solution.py:11
  14.0 0.7 multiply_exponential_fusion
  14.8 14.3 %all-to-all-done = bf16[4,128,1024]{1,2,0:T(8,128)(2,1)S(1)} async-done(((bf16[4,128,1024]{1,2,0:T(8,128)(2,1)}), bf16[4,128,1024]{1,2,0:T(8,128)(2,1)S(1)}, u32[]{:S(2)}, u32[]{:S(2)}) %all-to-all-start) | async-done | bytes 1048608 | tf_op jit(solution)/shard_map/all_to_all | solution.py:11
  29.1 74.1 %all-gather.5.cloned.1.call-done = bf16[4096,3,1024]{2,0,1:T(8,128)(2,1)} async-done(((bf16[128,3,1024]{2,0,1:T(8,128)(2,1)}), bf16[4096,3,1024]{2,0,1:T(8,128)(2,1)}) %all-gather.5.cloned.1.call-update) | async-done | bytes 25165840 | tf_op jit(solution)/shard_map/all_gather | solution.py:50
  103.2 4.7 %fusion.27 = bf16[1,128,1024]{2,1,0:T(8,128)(2,1)S(1)} fusion(bf16[128,4096]{0,1:T(8,128)(2,1)S(1)} %bitcast.86, bf16[4096,3,1024]{2,0,1:T(8,128)(2,1)} %all-gather.5.cloned.1.call-done), kind=kOutput, calls=%fused_computation.36 | convolution fusion | flops 1073872896 | bytes 9699328 | tf_op jit(solution)/shard_map/dot_general | solution.py:52
  107.8 4.7 %fusion.28 = bf16[1,128,1024]{2,1,0:T(8,128)(2,1)S(1)} fusion(bf16[128,4096]{0,1:T(8,128)(2,1)S(1)} %bitcast.87, bf16[4096,3,1024]{2,0,1:T(8,128)(2,1)} %all-gather.5.cloned.1.call-done), kind=kOutput, calls=%fused_computation.37 | convolution fusion | flops 1073872896 | bytes 9699328 | tf_op jit(solution)/shard_map/dot_general | solution.py:52
  112.5 4.7 %fusion.29 = bf16[1,128,1024]{2,1,0:T(8,128)(2,1)S(1)} fusion(bf16[128,4096]{0,1:T(8,128)(2,1)S(1)} %bitcast.88, bf16[4096,3,1024]{2,0,1:T(8,128)(2,1)} %all-gather.5.cloned.1.call-done), kind=kOutput, calls=%fused_computation.38 | convolution fusion | flops 1073872896 | bytes 9699328 | tf_op jit(solution)/shard_map/dot_general | solution.py:52
  117.2 2.4 collective-permute-start
  119.6 0.2 copy.66
  119.8 4.5 %collective-permute-done = bf16[3,2,1024]{2,1,0:T(2,128)(2,1)S(1)} collective-permute-done((bf16[3,2,1024]{2,1,0:T(2,128)(2,1)S(1)}, bf16[3,2,1024]{2,1,0:T(2,128)(2,1)S(1)}, u32[]{:S(2)}, u32[]{:S(2)}) %collective-permute-start) | collective-permute-done | bytes 12320 | tf_op jit(solution)/shard_map/ppermute | solution.py:22
  124.4 0.2 maximum_maximum_fusion
  124.8 0.5 fusion.22
  125.3 1.1 copy-done
  126.4 0.8 copy.69
  127.2 14.8 %fusion.10 = f32[1024,4,16]{2,1,0:T(4,128)} fusion(f32[4,32,1024]{1,0,2:T(4,128)S(1)} %copy.69, f32[32]{0:T(128)S(1)} %iota_subtract_fusion, f32[16,1024]{0,1:T(8,128)S(1)} %copy.66), kind=kOutput, calls=%fused_computation.16 | convolution fusion | flops 25690112 | bytes 852096 | tf_op jit(solution)/shard_map/spc,bsc->bpc/dot_general | solution.py:75
  142.1 1.9 copy.71
  144.1 0.6 slice.182
  144.8 1.0 copy.65
  145.9 15.3 %multiply_reduce_fusion = f32[32,1024]{0,1:T(8,128)S(1)} fusion(f32[16,1024]{0,1:T(8,128)S(1)} %copy.66, f32[16,1024]{0,1:T(8,128)} %copy.65), kind=kLoop, calls=%fused_computation.20 | loop fusion | flops 1540096 | bytes 262144 | tf_op jit(solution)/shard_map/reduce_sum | solution.py:69
  161.4 5.5 %gather_fusion = f32[1024,1024]{1,0:T(8,128)} fusion(f32[32,1024]{1,0:T(8,128)S(1)} %copy.67, s32[1024]{0:T(1024)S(1)} %broadcast_clamp_fusion), kind=kCustom, calls=%fused_computation | custom fusion | bytes 8392704 | tf_op jit(solution)/shard_map/gather | solution.py:71
  166.9 14.4 %copy.68 = f32[32,32,1024]{1,0,2:T(8,128)} copy(f32[32,32,1024]{2,1,0:T(8,128)} %bitcast.82) | data formatting | bytes 8388608 | tf_op jit(solution)/shard_map/gather | solution.py:71
  181.5 0.7 slice_add_fusion
  182.2 29.5 %fusion.1 = f32[1024,4,32]{2,1,0:T(4,128)} fusion(f32[4,32,1024]{1,0,2:T(4,128)S(1)} %copy.69, f32[32,32,1024]{1,0,2:T(8,128)} %copy.68, pred[32,32]{1,0:T(8,128)(4,1)S(1)} %subtract_compare_fusion), kind=kOutput, calls=%fused_computation.4 | convolution fusion | flops 51380224 | bytes 5243904 | tf_op jit(solution)/shard_map/tsc,bsc->btc/dot_general | solution.py:73
  211.7 30.1 %while.14 = (s32[]{:T(128)}, f32[16,1024]{1,0:T(8,128)S(1)}, s32[]{:T(128)}, f32[32,16,1024]{2,1,0:T(8,128)}, f32[32,16,1024]{2,1,0:T(8,128)}, /*index=5*/s32[]{:T(128)}, s32[]{:T(128)}) while((s32[]{:T(128)}, f32[16,1024]{1,0:T(8,128)S(1)}, s32[]{:T(128)}, f32[32,16,1024]{2,1,0:T(8,128)}, f32[32,16,1024]{2,1,0:T(8,128)}, ...), condition=%wide.region_2.3_spmd.clone, body=%wide.region_1.2_spmd.clone.sunk | while | flops 65540 | bytes 262253 | solution.py:39
  211.8 1.1 fusion.45
  212.9 0.9 fusion.45
  213.8 0.9 fusion.45
  214.7 0.9 fusion.45
  215.7 0.9 fusion.45
  216.6 0.9 fusion.45
  217.5 0.9 fusion.45
  218.5 0.9 fusion.45
  219.4 0.9 fusion.45
  220.3 0.9 fusion.45
  221.3 0.9 fusion.45
  222.2 0.9 fusion.45
  223.2 0.9 fusion.45
  224.1 0.9 fusion.45
  225.0 0.9 fusion.45
  226.0 0.9 fusion.45
  226.9 0.9 fusion.45
  227.8 0.9 fusion.45
  228.8 0.9 fusion.45
  229.7 0.9 fusion.45
  230.7 0.9 fusion.45
  231.6 0.9 fusion.45
  232.5 0.9 fusion.45
  233.5 0.9 fusion.45
  234.4 0.9 fusion.45
  235.3 0.9 fusion.45
  236.3 0.9 fusion.45
  237.2 0.9 fusion.45
  238.1 0.9 fusion.45
  239.1 0.9 fusion.45
  240.0 0.9 fusion.45
  241.0 0.9 fusion.45
  241.9 1.0 multiply_add_fusion
  242.9 1.7 copy.72
  244.7 12.9 %add_bitcast_fusion = f32[4,32,1024]{1,0,2:T(4,128)} fusion(f32[1024,4,32]{2,1,0:T(4,128)S(1)} %copy-done.2, f32[4,16,1024]{1,0,2:T(4,128)} %copy.72, f32[32]{0:T(128)S(1)} %iota_add_fusion, f32[16,1024]{0,1:T(8,128)S(1)} %copy.66, f32[16,1024]{0,1:T(8,128)S(1)} %copy-done.3), kind=kOutput, calls=%fused_computation.27 | convolution fusion | flops 26345472 | bytes 1441920 | tf_op jit(solution)/shard_map/tpc,bpc->btc/dot_general | solution.py:87
  257.5 2.0 copy.73
  259.6 0.9 fusion.31
  (59 shorter events, 1.0 us)
Async XLA Ops:
  6.5 96.6 %all-gather.5.cloned.1.call-start = ((), (), s32[]{:S(2)}) async-start(), calls=%async_computation.1 | async-start | bytes 25952256 | tf_op jit(solution)/shard_map/all_gather | solution.py:50
  7.3 6.8 %copy-start.6 = (f32[16,1024]{1,0:T(8,128)S(1)}, f32[16,1024]{1,0:T(8,128)}, u32[]{:S(2)}) copy-start(f32[16,1024]{1,0:T(8,128)} %param.11) | copy-start | bytes 196612
  7.3 7.5 %copy-start.14 = (f32[3,3,1024]{2,1,0:T(4,128)S(1)}, f32[3,3,1024]{2,1,0:T(4,128)}, u32[]{:S(2)}) copy-start(f32[3,3,1024]{2,1,0:T(4,128)} %param.10) | copy-start | bytes 110596
  9.6 19.6 %all-to-all-start = ((bf16[4,128,1024]{1,2,0:T(8,128)(2,1)}), bf16[4,128,1024]{1,2,0:T(8,128)(2,1)S(1)}, u32[]{:S(2)}, u32[]{:S(2)}) async-start(bf16[4,128,1024]{1,2,0:T(8,128)(2,1)} %stack.19), calls=%async_computation | async-start | bytes 2097152 | tf_op jit(solution)/shard_map/all_to_all | solution.py:11
  14.0 197.7 %all-gather.9.cloned.1.call-start = ((), (), s32[]{:S(2)}) async-start(), calls=%async_computation.3 | async-start | bytes 2162688 | tf_op jit(solution)/shard_map/all_gather | solution.py:27
  14.7 104.9 %copy-start.11 = (f32[16,1024]{1,0:T(8,128)}, f32[16,1024]{1,0:T(8,128)S(1)}, u32[]{:S(2)}) copy-start(f32[16,1024]{1,0:T(8,128)S(1)} %get-tuple-element.144) | copy-start | bytes 196612
  14.8 197.0 %all-gather.7.cloned.1.call-start = ((), (), s32[]{:S(2)}) async-start(), calls=%async_computation.2 | async-start | bytes 2162688 | tf_op jit(solution)/shard_map/all_gather | solution.py:27
  117.2 7.1 %collective-permute-start = (bf16[3,2,1024]{2,1,0:T(2,128)(2,1)S(1)}, bf16[3,2,1024]{2,1,0:T(2,128)(2,1)S(1)}, u32[]{:S(2)}, u32[]{:S(2)}) collective-permute-start(bf16[3,2,1024]{2,1,0:T(2,128)(2,1)S(1)} %pad_maximum_fusion.1), channel_id=1, source_target_pairs={{0,4},{4,8},{8,12},{12,16},{16,20},{20,24},{24,28},{28,32},{32,36}... | collective-permute-start | bytes 36872 | tf_op jit(solution)/shard_map/ppermute | solution.py:22
  125.2 1.1 copy-start
  142.1 2.8 %copy-start.13 = (f32[16,1024]{1,0:T(8,128)S(1)}, f32[16,1024]{1,0:T(8,128)}, u32[]{:S(2)}) copy-start(f32[16,1024]{1,0:T(8,128)} %param.12) | copy-start | bytes 196612
  144.0 0.8 copy-start.4
  144.1 0.8 copy-start.7
  144.1 0.8 copy-start.9
  166.9 14.5 %copy-start.5 = (f32[1024,4,16]{0,2,1:T(8,128)S(1)}, f32[1024,4,16]{0,2,1:T(8,128)}, u32[]{:S(2)}) copy-start(f32[1024,4,16]{0,2,1:T(8,128)} %copy-done.4) | copy-start | bytes 786436
  166.9 14.5 %copy-start.8 = (f32[1,16,1024]{2,1,0:T(8,128)S(1)}, f32[1,16,1024]{2,1,0:T(8,128)}, u32[]{:S(2)}) copy-start(f32[1,16,1024]{2,1,0:T(8,128)} %copy-done.7) | copy-start | bytes 196612
  166.9 14.5 %copy-start.10 = (f32[1,16,1024]{2,1,0:T(8,128)S(1)}, f32[1,16,1024]{2,1,0:T(8,128)}, u32[]{:S(2)}) copy-start(f32[1,16,1024]{2,1,0:T(8,128)} %copy-done.9) | copy-start | bytes 196612
  182.2 59.7 %copy-start.12 = (f32[16,1024]{1,0:T(8,128)S(1)}, f32[16,1024]{1,0:T(8,128)}, u32[]{:S(2)}) copy-start(f32[16,1024]{1,0:T(8,128)} %copy-done.11) | copy-start | bytes 196612
  211.7 32.9 %copy-start.2 = (f32[1024,4,32]{2,1,0:T(4,128)S(1)}, f32[1024,4,32]{2,1,0:T(4,128)}, u32[]{:S(2)}) copy-start(f32[1024,4,32]{2,1,0:T(4,128)} %fusion.1) | copy-start | bytes 1572868
  211.7 32.9 %copy-start.3 = (f32[16,1024]{0,1:T(8,128)S(1)}, f32[16,1024]{0,1:T(8,128)}, u32[]{:S(2)}) copy-start(f32[16,1024]{0,1:T(8,128)} %copy.65) | copy-start | bytes 196612
  257.5 2.0 copy-start.1
  257.5 2.0 copy-start.15
Sparse Core Ops, SparseCore 0:
  9.7 93.4 all-gather.4
  105.4 43.6 all-gather.8
  151.4 43.2 all-gather.6
